TPU v7x, 128 devices: a whole 4x4x4 slice. The times are simulated.
128 devices in a mesh: space: 16 (over x, z), mem: 8 (over y, core).
Axes of the slice: x: 4, y: 4, z: 4, core: 2. Of those that a mesh axis runs over, the one named last changes fastest.
Arguments:
- ensemble_state: bfloat16 [256, 1024, 256], P('mem', 'space'), may hold values from -6 to 6
- obs_ens: bfloat16 [256, 1024, 128], P('mem', 'space'), may hold values from -6 to 6
- innovation: float32 [1024, 128], P('space'), may hold values from -6 to 6
- obs_prec: float32 [1024, 128], P('space'), may hold values from 0.25 to 2
- block_list: int32 [1024, 8], P('space'), may hold values from 0 to 1023, as said below
- block_count: int32 [1024], P('space'), may hold values from 1 to 8
- loc_weight: float32 [1024, 8], P('space'), may hold values from 0.1 to 1
- prior_weight: float32 [1024, 256], P('space'), may hold values from 0.1 to 10, as said below
Outputs:
- analysis: bfloat16 [256, 1024, 256], P('mem', 'space')
Inputs may be any that keep to these rules, and one draw needn't show every extreme that they name: `block_list`: among the 64 entries of the regions r with the same r // 8, at most 6 name blocks b with the same b // 64, and exactly 6 do for one such value. `prior_weight`: Positive.
All inputs are finite; a program needn't handle non-finite values.
Results may differ from a plain program's by a relative error of at most 0.012.
Values may be sent and summed in bfloat16 or wider, within the bound.
A program may use at most 128 MiB of HBM per device.

v0:
```python
import jax
import jax.numpy as jnp
from jax import lax
from jax.sharding import PartitionSpec as P

INFLATION = 1.1


def transform(gram_blocks, projection, prior_rows):
    highest = lax.Precision.HIGHEST
    members = gram_blocks.shape[-1]
    shares = prior_rows / jnp.sum(prior_rows, axis=1, keepdims=True)
    root_q = jnp.sqrt(members * shares)
    left_term = jnp.einsum("rk,rkj->rj", shares, gram_blocks, precision=highest)
    centred = gram_blocks - left_term[:, None, :]
    right_term = jnp.einsum("rik,rk->ri", centred, shares, precision=highest)
    centred = centred - right_term[:, :, None]
    identity = jnp.eye(members, dtype=jnp.float32)
    system = (
        root_q[:, :, None] * centred * root_q[:, None, :] + (members - 1) / INFLATION * identity
    )
    vector = root_q * (projection - jnp.sum(shares * projection, axis=1, keepdims=True))
    factor = jnp.linalg.cholesky(system)
    inverse = jax.scipy.linalg.solve_triangular(
        factor, jnp.broadcast_to(identity, system.shape), lower=True
    )
    solved = jnp.einsum("rij,rj->ri", inverse, vector, precision=highest)
    weights = jnp.einsum("rji,rj->ri", inverse, solved, precision=highest)
    spread = jnp.sqrt(members - 1.0) * jnp.transpose(inverse, (0, 2, 1))
    mixing = root_q[:, :, None] * (weights[:, :, None] + spread)
    mixing = (
        mixing - shares[:, :, None] * jnp.sum(mixing, axis=1, keepdims=True) + shares[:, :, None]
    )
    return mixing


def body(
    ensemble_state, obs_ens, innovation, obs_prec, block_list, block_count, loc_weight, prior_weight
):
    spaces = lax.axis_size("space")
    mem_count = lax.axis_size("mem")
    members_dev = ensemble_state.shape[0]
    members = members_dev * mem_count
    regions_dev = ensemble_state.shape[1]
    group_size = regions_dev // mem_count
    blocks_dev = obs_ens.shape[1]
    obs_width = obs_ens.shape[2]
    slot_count = block_list.shape[1]
    entries = group_size * slot_count
    capacity = 3 * entries // (2 * spaces)
    mem_index = lax.axis_index("mem")
    first_row = mem_index * group_size
    block_ids = lax.dynamic_slice_in_dim(block_list, first_row, group_size, 0).reshape(entries)
    counts = lax.dynamic_slice_in_dim(block_count, first_row, group_size, 0)
    loc_rows = lax.dynamic_slice_in_dim(loc_weight, first_row, group_size, 0)
    prior_rows = lax.dynamic_slice_in_dim(prior_weight, first_row, group_size, 0)
    target = block_ids // blocks_dev
    local_ids = block_ids % blocks_dev
    onehot = (target[:, None] == jnp.arange(spaces, dtype=jnp.int32)[None, :]).astype(jnp.int32)
    slot_rank = jnp.sum(onehot * jnp.cumsum(onehot, axis=0), axis=1) - 1
    request_table = jnp.zeros((spaces, capacity), jnp.int32).at[target, slot_rank].set(local_ids)
    wanted = jnp.broadcast_to(request_table[:, None, :], (spaces, mem_count, capacity))
    wanted = wanted.reshape(spaces * mem_count, capacity)
    asked_ids = lax.all_to_all(wanted, ("space", "mem"), split_axis=0, concat_axis=0, tiled=True)
    outgoing = jnp.take(obs_ens, asked_ids, axis=1)
    arrived = lax.all_to_all(outgoing, ("space", "mem"), split_axis=1, concat_axis=1, tiled=True)
    arrived = arrived.reshape(members_dev, spaces, mem_count, capacity, obs_width)
    picked = arrived[:, target, :, slot_rank, :]
    picked = jnp.transpose(picked, (2, 1, 0, 3)).reshape(members, entries, obs_width)
    asked_grid = asked_ids.reshape(spaces, mem_count, capacity)
    from_peers = lax.dynamic_index_in_dim(asked_grid, mem_index, axis=1, keepdims=False)
    error_prec = jnp.take(obs_prec, from_peers, axis=0)
    error_innov = jnp.take(innovation, from_peers, axis=0)
    got_prec, got_innov = (
        lax.all_to_all(error_prec, "space", split_axis=0, concat_axis=0, tiled=True),
        lax.all_to_all(error_innov, "space", split_axis=0, concat_axis=0, tiled=True),
    )
    prec_rows = got_prec[target, slot_rank]
    innov_rows = got_innov[target, slot_rank]
    active = (jnp.arange(slot_count, dtype=jnp.int32)[None, :] < counts[:, None]).astype(
        jnp.float32
    )
    obs_weight = (active * loc_rows).reshape(entries)[:, None] * prec_rows
    obs_scale = jnp.sqrt(obs_weight)
    scaled = (picked.astype(jnp.float32) * obs_scale[None]).astype(jnp.bfloat16)
    shaped = scaled.reshape(members, group_size, slot_count, obs_width)
    gram_blocks = jnp.einsum("krlo,jrlo->rkj", shaped, shaped, preferred_element_type=jnp.float32)
    weighted_innov = (obs_scale * innov_rows).reshape(group_size, slot_count, obs_width)
    projection = jnp.einsum(
        "krlo,rlo->rk", shaped, weighted_innov, preferred_element_type=jnp.float32
    )
    mixing = transform(gram_blocks, projection, prior_rows)
    mix_high = mixing.astype(jnp.bfloat16)
    mix_low = (mixing - mix_high.astype(jnp.float32)).astype(jnp.bfloat16)
    mix_parts = jnp.concatenate([mix_high, mix_low], axis=2)
    region_states = lax.all_to_all(ensemble_state, "mem", split_axis=1, concat_axis=0, tiled=True)
    both_parts = jnp.einsum(
        "krp,rkj->jrp", region_states, mix_parts, preferred_element_type=jnp.float32
    )
    updated = (both_parts[:members] + both_parts[members:]).astype(jnp.bfloat16)
    return lax.all_to_all(updated, "mem", split_axis=0, concat_axis=1, tiled=True)


def solution(mesh):
    return jax.shard_map(
        body,
        mesh=mesh,
        in_specs=(
            P("mem", "space", None),
            P("mem", "space", None),
            P("space", None),
            P("space", None),
            P("space", None),
            P("space"),
            P("space", None),
            P("space", None),
        ),
        out_specs=P("mem", "space", None),
        check_vma=False,
    )
```

profile of v0, /device:TPU:1, one launch (start us, length us, event | category | flops | bytes accessed | tf_op | source)
XLA Modules:
  0.0 712.9 jit_solution(11391945641153206880)
XLA Ops:
  1.6 3.5 scatter_fusion
  5.8 11.5 %all-to-all-start = ((s32[128,1,6]{2,1,0:T(1,128)}), s32[128,1,6]{2,1,0:T(1,128)S(1)}, u32[]{:S(2)}, u32[]{:S(2)}) async-start(s32[128,1,6]{2,1,0:T(1,128)} %bitcast.3), calls=%async_computation | async-start | bytes 131072 | tf_op jit(solution)/shard_map/all_to_all | solution.py:64
  17.3 9.4 %all-to-all-done = s32[128,1,6]{2,1,0:T(1,128)S(1)} async-done(((s32[128,1,6]{2,1,0:T(1,128)}), s32[128,1,6]{2,1,0:T(1,128)S(1)}, u32[]{:S(2)}, u32[]{:S(2)}) %all-to-all-start) | async-done | bytes 3104 | tf_op jit(solution)/shard_map/all_to_all | solution.py:64
  27.0 1.4 gather_fusion.4
  29.8 9.7 %all_to_all.66 = f32[16,6,128]{2,1,0:T(8,128)S(1)} all-to-all(f32[16,6,128]{2,1,0:T(8,128)S(1)} %get-tuple-element.39), channel_id=1, replica_groups=mesh['space'=16,'mem'=8] {'space'}, dimensions={0} | all-to-all | bytes 98304 | tf_op jit(solution)/shard_map/all_to_all | solution.py:75
  39.6 3.5 all-to-all-start.3
  43.1 1.6 copy.140
  44.6 4.9 all-to-all-done.3
  49.5 6.6 all-to-all-start.4
  56.3 29.1 %gather_fusion = bf16[768,32,128]{2,0,1:T(8,128)(2,1)} fusion(bf16[32,64,128]{2,1,0:T(8,128)(2,1)S(1)} %copy-done, s32[1024]{0:T(1024)S(1)} %pad_clamp_fusion.1), kind=kCustom, calls=%fused_computation.2 | custom fusion | bytes 12585984 | tf_op jit(solution)/shard_map/jit(_take)/gather | solution.py:65
  85.4 6.8 copy.116
  92.3 3.5 select_bitcast_fusion
  95.8 6.3 all-to-all-start.1
  106.5 71.5 %all-to-all-done.1 = bf16[32,128,6,128]{3,0,2,1:T(8,128)(2,1)} async-done(((bf16[32,128,6,128]{3,0,2,1:T(8,128)(2,1)}), bf16[32,128,6,128]{3,0,2,1:T(8,128)(2,1)}, u32[]{:S(2)}, u32[]{:S(2)}) %all-to-all-start.1) | async-done | bytes 6291488 | tf_op jit(solution)/shard_map/all_to_all | solution.py:66
  178.0 9.5 %copy.118 = bf16[32,16,8,6,128]{4,2,3,1,0:T(8,128)(2,1)} copy(bf16[32,16,8,6,128]{4,0,3,2,1:T(8,128)(2,1)} %bitcast.8) | data formatting | bytes 12582912 | tf_op jit(solution)/shard_map/reshape | solution.py:67
  187.4 6.6 gather_fusion.1
  194.1 3.3 convert_bitcast_fusion
  197.3 13.6 %copy.119 = f32[8,32,64,128]{3,2,1,0:T(8,128)S(1)} copy(f32[8,32,64,128]{3,0,1,2:T(8,128)S(1)} %convert_bitcast_fusion) | data formatting | bytes 16777216 | tf_op jit(solution)/shard_map/convert_element_type | solution.py:85
  210.9 1.2 multiply_convert_fusion
  212.1 5.8 fusion.15
  217.9 2.3 fusion.1
  220.2 1.9 copy.127
  223.1 2.7 fusion.45
  225.8 1.3 fusion.13
  227.2 1.7 fusion.20
  228.8 2.9 copy.129
  231.7 2.2 fusion.12
  233.9 1.3 copy-done.5
  235.3 93.8 %custom-call.17 = f32[8,128,128]{2,1,0:T(8,128)S(1)} custom-call(f32[8,128,128]{2,1,0:T(8,128)S(1)} %cholesky.122), custom_call_target="Cholesky" | custom-call | tf_op jit(solution)/shard_map/jit(cholesky)/cholesky | solution.py:23
  329.3 79.2 %custom-call.18 = f32[8,1,128,128]{2,3,1,0:T(8,128)} custom-call(f32[8,1,128,128]{3,2,1,0:T(8,128)S(1)} %select_bitcast_fusion.1), custom_call_target="InvertDiagBlocksLowerTriangular" | custom-call | tf_op jit(solution)/shard_map/jit(cholesky)/cholesky | solution.py:23
  408.5 1.8 constant_dynamic-update-slice_fusion.1
  410.4 3.1 convolution_subtract_fusion.1
  413.4 94.8 %custom-call.19 = f32[8,128,128]{2,1,0:T(8,128)S(1)} custom-call(f32[8,128,128]{2,1,0:T(8,128)} %convolution_subtract_fusion.1), custom_call_target="Cholesky" | custom-call | tf_op jit(solution)/shard_map/jit(cholesky)/cholesky | solution.py:23
  508.5 1.2 copy-done.4
  509.7 1.9 select_select_fusion
  511.7 5.8 while.1
  512.3 2.3 bitcast_dynamic-update-slice_fusion.2
  515.2 2.2 bitcast_dynamic-update-slice_fusion.2
  517.4 158.6 %custom-call.20 = f32[8,2,128,128]{2,3,1,0:T(8,128)} custom-call(f32[8,2,128,128]{3,2,1,0:T(8,128)} %bitcast.159), custom_call_target="InvertDiagBlocksLowerTriangular" | custom-call | tf_op jit(solution)/shard_map/jit(_solve_triangular)/vmap()/triangular_solve | solution.py:24
  676.1 3.1 fusion.29
  679.1 2.6 copy.135
  681.7 2.4 convolution_subtract_fusion
  684.1 2.0 fusion.28
  686.1 1.2 fusion.26
  687.3 1.8 fusion.25
  689.2 1.7 subtract_convert_fusion
  692.5 18.8 %all_to_all.67 = bf16[256,8,256]{2,1,0:T(8,128)(2,1)S(1)} all-to-all(bf16[256,8,256]{2,1,0:T(8,128)(2,1)S(1)} %copy.143), channel_id=1, replica_groups=mesh['space'=16,'mem'=8] {'mem'}, dimensions={0} | all-to-all | bytes 2097152 | tf_op jit(solution)/shard_map/all_to_all | solution.py:101
  711.4 1.1 copy.196
  (90 shorter events, 12.8 us)
Async XLA Ops:
  0.0 56.3 %copy-start = (bf16[32,64,128]{2,1,0:T(8,128)(2,1)S(1)}, bf16[32,64,128]{2,1,0:T(8,128)(2,1)}, u32[]{:S(2)}) copy-start(bf16[32,64,128]{2,1,0:T(8,128)(2,1)} %param.11) | copy-start | bytes 1572868
  0.0 28.4 %copy-start.3 = (f32[64,128]{1,0:T(8,128)S(1)}, f32[64,128]{1,0:T(8,128)}, u32[]{:S(2)}) copy-start(f32[64,128]{1,0:T(8,128)} %param.12) | copy-start | bytes 98308
  0.0 43.0 %copy-start.8 = (bf16[32,64,256]{2,1,0:T(8,128)(2,1)S(1)}, bf16[32,64,256]{2,1,0:T(8,128)(2,1)}, u32[]{:S(2)}) copy-start(bf16[32,64,256]{2,1,0:T(8,128)(2,1)} %param.10) | copy-start | bytes 3145732
  5.8 20.9 %all-to-all-start = ((s32[128,1,6]{2,1,0:T(1,128)}), s32[128,1,6]{2,1,0:T(1,128)S(1)}, u32[]{:S(2)}, u32[]{:S(2)}) async-start(s32[128,1,6]{2,1,0:T(1,128)} %bitcast.3), calls=%async_computation | async-start | bytes 131072 | tf_op jit(solution)/shard_map/all_to_all | solution.py:64
  39.6 10.0 %all-to-all-start.3 = ((f32[16,6,128]{2,1,0:T(8,128)}), f32[16,6,128]{2,1,0:T(8,128)S(1)}, u32[]{:S(2)}, u32[]{:S(2)}) async-start(f32[16,6,128]{2,1,0:T(8,128)} %get-tuple-element.40), calls=%async_computation.3 | async-start | bytes 131072 | tf_op jit(solution)/shard_map/all_to_all | solution.py:76
  49.5 46.3 %all-to-all-start.4 = ((bf16[32,64,256]{2,0,1:T(8,128)(2,1)}), bf16[32,64,256]{2,0,1:T(8,128)(2,1)S(1)}, u32[]{:S(2)}, u32[]{:S(2)}) async-start(bf16[32,64,256]{2,0,1:T(8,128)(2,1)} %copy.140), calls=%async_computation.4 | async-start | bytes 2097152 | tf_op jit(solution)/shard_map/all_to_all | solution.py:96
  95.8 6.4 copy-start.10
  95.8 6.4 copy-start.9
  95.8 82.1 %all-to-all-start.1 = ((bf16[32,128,6,128]{3,0,2,1:T(8,128)(2,1)}), bf16[32,128,6,128]{3,0,2,1:T(8,128)(2,1)}, u32[]{:S(2)}, u32[]{:S(2)}) async-start(bf16[32,128,6,128]{3,0,2,1:T(8,128)(2,1)} %select_bitcast_fusion), calls=%async_computation.1 | async-start | bytes 12582912 | tf_op jit(solution)/shard_map/all_to_all | solution.py:66
  233.9 1.3 copy-start.5
  508.3 1.3 copy-start.4
  681.7 2.4 copy-start.7
  681.7 4.4 copy-start.2
  689.1 1.7 copy-start.6
  691.9 20.5 %copy-start.1 = (bf16[32,64,128]{2,1,0:T(8,128)(2,1)S(1)}, bf16[32,64,128]{2,1,0:T(8,128)(2,1)}, u32[]{:S(2)}) copy-start(bf16[32,64,128]{2,1,0:T(8,128)(2,1)} %param.11) | copy-start | bytes 1572868
where the time goes:
time: 722 us; the launch traced here: 713 us
  other arithmetic  446 us (62%)
  local copies, waits for them, and re-layouts  95.8 us (13%)
  waiting for transfers between devices  85.8 us (12%)
  blocking collectives  28.5 us (4%)
  matrix products  28.4 us (4%)
  starting transfers between devices  28 us (4%)
    another operation x9, other arithmetic, transform(): factor = jnp.linalg.cholesky(system)  268 us
    another operation x4, other arithmetic, transform(): jax.scipy.linalg.solve_triangular(factor, jnp.broadcast_to(identity, syst...  161 us
    all_to_all x1, waiting for transfers between devices, body(): lax.all_to_all(outgoing, ('space', 'mem'), split_axis=1, concat_axis=1, t...  71.5 us
    gather x2, local copies, waits for them, and re-layouts, body(): outgoing = jnp.take(obs_ens, asked_ids, axis=1)  35.9 us
    all_to_all x1, blocking collectives, body(): lax.all_to_all(updated, 'mem', split_axis=0, concat_axis=1, tiled=True)  18.8 us
  transfers between devices with their start and end apart: 4, of which 3 were waited for; matrix products, arithmetic and copies ran while one was open for 6% of the time, Pallas kernels for 0%

commit v1 on v0

--- a/solution.py
+++ b/solution.py
@@ -2,6 +2,7 @@
 import jax.numpy as jnp
 from jax import lax
 from jax.sharding import PartitionSpec as P
+from jax.lax import all_to_all, axis_size
 
 INFLATION = 1.1
 
@@ -98,7 +99,9 @@
         "krp,rkj->jrp", region_states, mix_parts, preferred_element_type=jnp.float32
     )
     updated = (both_parts[:members] + both_parts[members:]).astype(jnp.bfloat16)
-    return lax.all_to_all(updated, "mem", split_axis=0, concat_axis=1, tiled=True)
+    return jnp.concatenate(
+        all_to_all(jnp.stack(jnp.split(updated, axis_size("mem"), axis=0), 0), "mem", 0, 0), 1
+    )
 
 
 def solution(mesh):

time: 722 us -> 721 us (level)
    another operation x9 -> x10, other arithmetic: 268 us -> 268 us  [transform(): factor = jnp.linalg.cholesky(system)]
where the time goes in v1:
time: 721 us; the launch traced here: 712 us
  other arithmetic  446 us (62%)
  local copies, waits for them, and re-layouts  94.9 us (13%)
  waiting for transfers between devices  85.8 us (12%)
  blocking collectives  28.7 us (4%)
  matrix products  28.4 us (4%)
  starting transfers between devices  28 us (4%)
    another operation x10, other arithmetic, transform(): factor = jnp.linalg.cholesky(system)  268 us
    another operation x4, other arithmetic, transform(): jax.scipy.linalg.solve_triangular(factor, jnp.broadcast_to(identity, syst...  161 us
    all_to_all x1, waiting for transfers between devices, body(): lax.all_to_all(outgoing, ('space', 'mem'), split_axis=1, concat_axis=1, t...  71.5 us
    gather x2, local copies, waits for them, and re-layouts, body(): outgoing = jnp.take(obs_ens, asked_ids, axis=1)  36 us
    all_to_all x1, blocking collectives, body(): all_to_all(jnp.stack(jnp.split(updated, axis_size('mem'), axis=0), 0), 'm...  19 us
  transfers between devices with their start and end apart: 4, of which 3 were waited for; matrix products, arithmetic and copies ran while one was open for 6% of the time, Pallas kernels for 0%

profile of v1, /device:TPU:1, one launch (start us, length us, event | category | flops | bytes accessed | tf_op | source)
XLA Modules:
  0.0 712.4 jit_solution(5923969030909888357)
XLA Ops:
  1.6 3.5 scatter_fusion
  5.8 11.5 %all-to-all-start = ((s32[128,1,6]{2,1,0:T(1,128)}), s32[128,1,6]{2,1,0:T(1,128)S(1)}, u32[]{:S(2)}, u32[]{:S(2)}) async-start(s32[128,1,6]{2,1,0:T(1,128)} %bitcast.3), calls=%async_computation | async-start | bytes 131072 | tf_op jit(solution)/shard_map/all_to_all | solution.py:65
  17.3 9.4 %all-to-all-done = s32[128,1,6]{2,1,0:T(1,128)S(1)} async-done(((s32[128,1,6]{2,1,0:T(1,128)}), s32[128,1,6]{2,1,0:T(1,128)S(1)}, u32[]{:S(2)}, u32[]{:S(2)}) %all-to-all-start) | async-done | bytes 3104 | tf_op jit(solution)/shard_map/all_to_all | solution.py:65
  29.3 9.7 %all_to_all.53 = f32[16,6,128]{2,1,0:T(8,128)S(1)} all-to-all(f32[16,6,128]{2,1,0:T(8,128)S(1)} %get-tuple-element.39), channel_id=1, replica_groups=mesh['space'=16,'mem'=8] {'space'}, dimensions={0} | all-to-all | bytes 98304 | tf_op jit(solution)/shard_map/all_to_all | solution.py:76
  39.0 3.5 all-to-all-start.3
  42.5 1.6 copy.139
  44.0 4.9 all-to-all-done.3
  48.9 6.6 all-to-all-start.4
  55.6 29.2 %gather_fusion = bf16[768,32,128]{2,0,1:T(8,128)(2,1)} fusion(bf16[32,64,128]{2,1,0:T(8,128)(2,1)S(1)} %copy-done, s32[1024]{0:T(1024)S(1)} %get-tuple-element.46), kind=kCustom, calls=%fused_computation.2 | custom fusion | bytes 12585984 | tf_op jit(solution)/shard_map/jit(_take)/gather | solution.py:66
  84.8 6.8 copy.115
  91.6 3.5 select_bitcast_fusion
  95.2 6.3 all-to-all-start.1
  104.8 1.1 copy.140
  105.8 71.5 %all-to-all-done.1 = bf16[32,128,6,128]{3,0,2,1:T(8,128)(2,1)} async-done(((bf16[32,128,6,128]{3,0,2,1:T(8,128)(2,1)}), bf16[32,128,6,128]{3,0,2,1:T(8,128)(2,1)}, u32[]{:S(2)}, u32[]{:S(2)}) %all-to-all-start.1) | async-done | bytes 6291488 | tf_op jit(solution)/shard_map/all_to_all | solution.py:67
  177.3 9.5 %copy.117 = bf16[32,16,8,6,128]{4,2,3,1,0:T(8,128)(2,1)} copy(bf16[32,16,8,6,128]{4,0,3,2,1:T(8,128)(2,1)} %bitcast.8) | data formatting | bytes 12582912 | tf_op jit(solution)/shard_map/reshape | solution.py:68
  186.8 6.6 gather_fusion.1
  193.4 3.3 convert_bitcast_fusion
  196.7 13.6 %copy.118 = f32[8,32,64,128]{3,2,1,0:T(8,128)S(1)} copy(f32[8,32,64,128]{3,0,1,2:T(8,128)S(1)} %convert_bitcast_fusion) | data formatting | bytes 16777216 | tf_op jit(solution)/shard_map/convert_element_type | solution.py:86
  210.2 1.2 multiply_convert_fusion
  211.4 5.8 fusion.15
  217.3 2.3 fusion.1
  219.6 1.9 copy.126
  222.4 2.7 fusion.53
  225.2 1.3 fusion.13
  226.5 1.7 fusion.20
  228.2 2.9 copy.128
  231.1 2.2 fusion.12
  233.3 1.3 copy-done.6
  234.6 93.8 %custom-call.17 = f32[8,128,128]{2,1,0:T(8,128)S(1)} custom-call(f32[8,128,128]{2,1,0:T(8,128)S(1)} %cholesky.122), custom_call_target="Cholesky" | custom-call | tf_op jit(solution)/shard_map/jit(cholesky)/cholesky | solution.py:24
  328.7 79.2 %custom-call.18 = f32[8,1,128,128]{2,3,1,0:T(8,128)} custom-call(f32[8,1,128,128]{3,2,1,0:T(8,128)S(1)} %select_bitcast_fusion.1), custom_call_target="InvertDiagBlocksLowerTriangular" | custom-call | tf_op jit(solution)/shard_map/jit(cholesky)/cholesky | solution.py:24
  407.9 1.8 constant_dynamic-update-slice_fusion.1
  409.7 3.1 convolution_subtract_fusion.1
  412.8 94.8 %custom-call.19 = f32[8,128,128]{2,1,0:T(8,128)S(1)} custom-call(f32[8,128,128]{2,1,0:T(8,128)} %convolution_subtract_fusion.1), custom_call_target="Cholesky" | custom-call | tf_op jit(solution)/shard_map/jit(cholesky)/cholesky | solution.py:24
  508.0 1.1 copy-done.5
  509.0 1.9 select_select_fusion
  511.0 5.7 while.1
  511.6 2.3 bitcast_dynamic-update-slice_fusion.2
  514.5 2.2 bitcast_dynamic-update-slice_fusion.2
  516.7 158.6 %custom-call.20 = f32[8,2,128,128]{2,3,1,0:T(8,128)} custom-call(f32[8,2,128,128]{3,2,1,0:T(8,128)} %bitcast.188), custom_call_target="InvertDiagBlocksLowerTriangular" | custom-call | tf_op jit(solution)/shard_map/jit(_solve_triangular)/vmap()/triangular_solve | solution.py:25
  675.4 3.1 fusion.29
  678.5 2.6 copy.134
  681.0 2.4 convolution_subtract_fusion
  683.4 2.0 fusion.28
  685.4 1.2 fusion.26
  686.6 1.8 fusion.25
  688.5 1.7 subtract_convert_fusion
  691.4 19.0 %all_to_all.54 = bf16[8,32,8,256]{3,1,2,0:T(8,128)(2,1)S(1)} all-to-all(bf16[8,32,8,256]{3,1,2,0:T(8,128)(2,1)S(1)} %fusion.37), channel_id=1, replica_groups=mesh['space'=16,'mem'=8] {'mem'}, dimensions={0} | all-to-all | bytes 2097152 | tf_op jit(solution)/shard_map/all_to_all | solution.py:103
  710.4 1.6 copy.142
  (99 shorter events, 11.9 us)
Async XLA Ops:
  0.0 55.6 %copy-start = (bf16[32,64,128]{2,1,0:T(8,128)(2,1)S(1)}, bf16[32,64,128]{2,1,0:T(8,128)(2,1)}, u32[]{:S(2)}) copy-start(bf16[32,64,128]{2,1,0:T(8,128)(2,1)} %param.11) | copy-start | bytes 1572868
  0.0 27.2 %copy-start.3 = (f32[64,128]{1,0:T(8,128)S(1)}, f32[64,128]{1,0:T(8,128)}, u32[]{:S(2)}) copy-start(f32[64,128]{1,0:T(8,128)} %param.13) | copy-start | bytes 98308
  0.0 27.8 %copy-start.4 = (f32[64,128]{1,0:T(8,128)S(1)}, f32[64,128]{1,0:T(8,128)}, u32[]{:S(2)}) copy-start(f32[64,128]{1,0:T(8,128)} %param.12) | copy-start | bytes 98308
  0.0 42.5 %copy-start.9 = (bf16[32,64,256]{2,1,0:T(8,128)(2,1)S(1)}, bf16[32,64,256]{2,1,0:T(8,128)(2,1)}, u32[]{:S(2)}) copy-start(bf16[32,64,256]{2,1,0:T(8,128)(2,1)} %param.10) | copy-start | bytes 3145732
  5.8 20.9 %all-to-all-start = ((s32[128,1,6]{2,1,0:T(1,128)}), s32[128,1,6]{2,1,0:T(1,128)S(1)}, u32[]{:S(2)}, u32[]{:S(2)}) async-start(s32[128,1,6]{2,1,0:T(1,128)} %bitcast.3), calls=%async_computation | async-start | bytes 131072 | tf_op jit(solution)/shard_map/all_to_all | solution.py:65
  39.0 10.0 %all-to-all-start.3 = ((f32[16,6,128]{2,1,0:T(8,128)}), f32[16,6,128]{2,1,0:T(8,128)S(1)}, u32[]{:S(2)}, u32[]{:S(2)}) async-start(f32[16,6,128]{2,1,0:T(8,128)} %get-tuple-element.40), calls=%async_computation.3 | async-start | bytes 131072 | tf_op jit(solution)/shard_map/all_to_all | solution.py:77
  48.9 46.2 %all-to-all-start.4 = ((bf16[32,64,256]{2,0,1:T(8,128)(2,1)}), bf16[32,64,256]{2,0,1:T(8,128)(2,1)S(1)}, u32[]{:S(2)}, u32[]{:S(2)}) async-start(bf16[32,64,256]{2,0,1:T(8,128)(2,1)} %copy.139), calls=%async_computation.4 | async-start | bytes 2097152 | tf_op jit(solution)/shard_map/all_to_all | solution.py:97
  95.2 6.4 copy-start.11
  95.2 6.4 copy-start.10
  95.2 82.1 %all-to-all-start.1 = ((bf16[32,128,6,128]{3,0,2,1:T(8,128)(2,1)}), bf16[32,128,6,128]{3,0,2,1:T(8,128)(2,1)}, u32[]{:S(2)}, u32[]{:S(2)}) async-start(bf16[32,128,6,128]{3,0,2,1:T(8,128)(2,1)} %select_bitcast_fusion), calls=%async_computation.1 | async-start | bytes 12582912 | tf_op jit(solution)/shard_map/all_to_all | solution.py:67
  233.3 1.3 copy-start.6
  507.7 1.3 copy-start.5
  681.0 2.4 copy-start.8
  681.0 4.4 copy-start.2
  688.5 1.7 copy-start.7
  691.4 20.5 %copy-start.1 = (bf16[32,64,128]{2,1,0:T(8,128)(2,1)S(1)}, bf16[32,64,128]{2,1,0:T(8,128)(2,1)}, u32[]{:S(2)}) copy-start(bf16[32,64,128]{2,1,0:T(8,128)(2,1)} %param.11) | copy-start | bytes 1572868
